TPU v7x, 256 devices: a whole 4x4x8 slice. The times are simulated.
256 devices in a mesh: seq: 64 (over y, z, core), tp: 4 (over x).
Axes of the slice: x: 4, y: 4, z: 8, core: 2. Of those that a mesh axis runs over, the one named last changes fastest.
Arguments:
- inputs: bfloat16 [4, 4, 1024], P(None, None, 'tp'), may hold values from -64 to 64
- attention_gain: bfloat16 [1024], replicated, may hold values from 0.099609375 to 1.8984375
- forward_gain: bfloat16 [1024], replicated, may hold values from 0.099609375 to 1.8984375
- query_weight: bfloat16 [1024, 1024], P(None, 'tp'), may hold values from -0.1875 to 0.1875
- key_weight: bfloat16 [1024, 1024], P(None, 'tp'), may hold values from -0.1875 to 0.1875
- value_weight: bfloat16 [1024, 1024], P(None, 'tp'), may hold values from -0.1875 to 0.1875
- output_weight: bfloat16 [1024, 1024], P('tp'), may hold values from -0.1875 to 0.1875
- gate_weight: bfloat16 [1024, 4096], P(None, 'tp'), may hold values from -0.1875 to 0.1875
- up_weight: bfloat16 [1024, 4096], P(None, 'tp'), may hold values from -0.1875 to 0.1875
- down_weight: bfloat16 [4096, 1024], P('tp'), may hold values from -0.09375 to 0.09375
- variate_bias: float32 [2, 16], replicated, may hold values from -256 to 256
- cache_keys: bfloat16 [4, 32768, 1024], P(None, 'seq', 'tp'), may hold values from -15 to 15
- cache_values: bfloat16 [4, 32768, 1024], P(None, 'seq', 'tp'), may hold values from -12 to 12
- cache_variates: int32 [4, 32768], P(None, 'seq'), may hold values from 0 to 7
- cache_mask: int32 [4, 32768], P(None, 'seq'), may hold values 0 or 1
- cache_lengths: int32 [4], replicated, may hold values from 1 to 32768, as said below
- fresh_flags: int32 [4], replicated, may hold values 0 or 1
- new_variates: int32 [4, 4], replicated, may hold values from 0 to 7
- new_times: int32 [4, 4], replicated, may hold values from 0 to 32771
Outputs:
- hidden_states: bfloat16 [4, 4, 1024], P(None, None, 'tp')
- new_keys: bfloat16 [4, 4, 1024], P(None, None, 'tp')
- new_values: bfloat16 [4, 4, 1024], P(None, None, 'tp')
Inputs may be any that keep to these rules, and one draw needn't show every extreme that they name: `cache_lengths`: some request has exactly 32768 filled positions.
All inputs are finite; a program needn't handle non-finite values. No bound on the sum of `cache_mask` on one device may be relied on, other than what follows from the above.
Results may differ from a plain program's by a relative error of at most 0.014.
Values may be sent and summed in bfloat16 or wider, within the bound.
A program may use at most 64 MiB of HBM per device.

v0:
```python
import math
import jax
import jax.numpy as jnp
from jax import lax
from jax.sharding import PartitionSpec as P

D = 1024
HEAD_DIM = 64
STEPS = 4
epsilon = 1e-05


def rotated(blocks, times):
    half = blocks.shape[-1] // 2
    ladder = jnp.arange(half, dtype=jnp.float32) * (2.0 / blocks.shape[-1])
    inverse = jnp.exp(-math.log(10000.0) * ladder)
    angles = times.astype(jnp.float32)[:, None] * inverse[None, :]
    cosine = jnp.cos(angles)[:, None, :]
    sine = jnp.sin(angles)[:, None, :]
    first = blocks[..., :half]
    second = blocks[..., half:]
    return jnp.concatenate(
        [first * cosine - second * sine, second * cosine + first * sine], axis=-1
    )


def join_parts(earlier, later):
    peak = jnp.maximum(earlier[0], later[0])
    factor_one = jnp.exp(earlier[0] - peak)
    factor_two = jnp.exp(later[0] - peak)
    totals = earlier[1] * factor_one + later[1] * factor_two
    repeat_by = earlier[2].shape[-1] // earlier[0].shape[-1]
    sums = earlier[2] * jnp.repeat(factor_one, repeat_by, axis=1) + later[2] * jnp.repeat(
        factor_two, repeat_by, axis=1
    )
    return (peak, totals, sums)


def on_device(
    inputs,
    attention_gain,
    forward_gain,
    query_weight,
    key_weight,
    value_weight,
    output_weight,
    gate_weight,
    up_weight,
    down_weight,
    variate_bias,
    cache_keys,
    cache_values,
    cache_variates,
    cache_mask,
    cache_lengths,
    fresh_flags,
    new_variates,
    new_times,
):
    local_width = query_weight.shape[1]
    local_heads = local_width // HEAD_DIM
    requests = inputs.shape[0]
    columns = inputs.shape[2]
    span = cache_keys.shape[1]
    scale = 1.0 / math.sqrt(HEAD_DIM)
    column_start = lax.axis_index("tp") * columns
    head_start = lax.axis_index("tp") * local_heads
    bias_local = lax.dynamic_slice_in_dim(variate_bias, head_start, local_heads, 1)
    same_bias = bias_local[0]
    other_bias = bias_local[1]
    positions = lax.axis_index("seq") * span + jnp.arange(span, dtype=jnp.int32)
    usable = (
        (positions[None, :] < cache_lengths[:, None])
        & (cache_mask == 1)
        & (fresh_flags[:, None] == 0)
    )
    key_blocks = cache_keys.reshape(requests, span, local_heads, HEAD_DIM)
    value_blocks = cache_values.reshape(requests, span, local_heads, HEAD_DIM)
    gain_first = attention_gain.astype(jnp.float32)[None, :]
    gain_second = forward_gain.astype(jnp.float32)[None, :]
    gain_first_local = lax.dynamic_slice_in_dim(gain_first, column_start, columns, 1)
    gain_second_local = lax.dynamic_slice_in_dim(gain_second, column_start, columns, 1)
    hidden_list = []
    key_list = []
    value_list = []
    for step_index in range(STEPS):
        current_low = inputs[:, step_index, :]
        current_local = current_low.astype(jnp.float32)
        square_sum = lax.psum(jnp.sum(current_local * current_local, axis=1), "tp")
        inverse_rms = lax.rsqrt(square_sum / D + epsilon)
        normed_local = (current_local * inverse_rms[:, None] * gain_first_local).astype(
            jnp.bfloat16
        )
        normed = lax.all_gather(normed_local, "tp", axis=1, tiled=True)
        query_full = jnp.dot(normed, query_weight, preferred_element_type=jnp.float32)
        key_full = jnp.dot(normed, key_weight, preferred_element_type=jnp.float32)
        value_full = jnp.dot(normed, value_weight, preferred_element_type=jnp.float32)
        times_now = new_times[:, step_index]
        queries_now = rotated(
            query_full.reshape(requests, local_heads, HEAD_DIM), times_now
        ).astype(jnp.bfloat16)
        keys_now = rotated(key_full.reshape(requests, local_heads, HEAD_DIM), times_now).astype(
            jnp.bfloat16
        )
        values_now = value_full.reshape(requests, local_heads, HEAD_DIM).astype(jnp.bfloat16)
        key_list.append(keys_now)
        value_list.append(values_now)
        variate_now = new_variates[:, step_index]
        same_cache = cache_variates == variate_now[:, None]
        scores = (
            jnp.einsum("rhe,rche->rhc", queries_now, key_blocks, preferred_element_type=jnp.float32)
            * scale
        )
        scores = scores + jnp.where(
            same_cache[:, None, :], same_bias[None, :, None], other_bias[None, :, None]
        )
        scores = jnp.where(usable[:, None, :], scores, -1e30)
        local_peak = jnp.max(scores, axis=2)
        raw = jnp.where(usable[:, None, :], jnp.exp(scores - local_peak[:, :, None]), 0.0)
        local_total = jnp.sum(raw, axis=2)
        local_sum = jnp.einsum(
            "rhc,rche->rhe",
            raw.astype(jnp.bfloat16),
            value_blocks,
            preferred_element_type=jnp.float32,
        ).reshape(requests, local_width)
        peak_all = lax.pmax(local_peak, "seq")
        factor = jnp.exp(local_peak - peak_all)
        totals_all, sums_all = lax.psum(
            (local_total * factor, local_sum * jnp.repeat(factor, HEAD_DIM, axis=1)), "seq"
        )
        merged = (peak_all, totals_all, sums_all)
        fresh_keys = jnp.stack(key_list, axis=1)
        fresh_values = jnp.stack(value_list, axis=1)
        same_new = new_variates[:, : step_index + 1] == variate_now[:, None]
        new_scores = (
            jnp.einsum("rhe,rshe->rhs", queries_now, fresh_keys, preferred_element_type=jnp.float32)
            * scale
        )
        new_scores = new_scores + jnp.where(
            same_new[:, None, :], same_bias[None, :, None], other_bias[None, :, None]
        )
        new_peak = jnp.max(new_scores, axis=2)
        new_raw = jnp.exp(new_scores - new_peak[:, :, None])
        new_total = jnp.sum(new_raw, axis=2)
        new_sum = jnp.einsum(
            "rhs,rshe->rhe",
            new_raw.astype(jnp.bfloat16),
            fresh_values,
            preferred_element_type=jnp.float32,
        ).reshape(requests, local_width)
        joined = join_parts(merged, (new_peak, new_total, new_sum))
        attention = (joined[2] / jnp.repeat(joined[1], HEAD_DIM, axis=1)).astype(jnp.bfloat16)
        partial_out = jnp.dot(attention, output_weight, preferred_element_type=jnp.float32)
        projected_local = lax.psum_scatter(partial_out, "tp", scatter_dimension=1, tiled=True)
        middle_local = (current_local + projected_local).astype(jnp.bfloat16).astype(jnp.float32)
        middle_sum = lax.psum(jnp.sum(middle_local * middle_local, axis=1), "tp")
        second_rms = lax.rsqrt(middle_sum / D + epsilon)
        normed_two_local = (middle_local * second_rms[:, None] * gain_second_local).astype(
            jnp.bfloat16
        )
        normed_two = lax.all_gather(normed_two_local, "tp", axis=1, tiled=True)
        gate_part = jnp.dot(normed_two, gate_weight, preferred_element_type=jnp.float32)
        up_part = jnp.dot(normed_two, up_weight, preferred_element_type=jnp.float32)
        activated = (jax.nn.silu(gate_part) * up_part).astype(jnp.bfloat16)
        down_part = jnp.dot(activated, down_weight, preferred_element_type=jnp.float32)
        forward = lax.psum_scatter(down_part, "tp", scatter_dimension=1, tiled=True)
        hidden_list.append((middle_local + forward).astype(jnp.bfloat16))
    hidden_states = jnp.stack(hidden_list, axis=1)
    new_keys = jnp.stack(key_list, axis=1).reshape(requests, STEPS, local_width)
    new_values = jnp.stack(value_list, axis=1).reshape(requests, STEPS, local_width)
    return (hidden_states, new_keys, new_values)


def solution(mesh):
    return jax.shard_map(
        on_device,
        mesh=mesh,
        in_specs=(
            P(None, None, "tp"),
            P(),
            P(),
            P(None, "tp"),
            P(None, "tp"),
            P(None, "tp"),
            P("tp", None),
            P(None, "tp"),
            P(None, "tp"),
            P("tp", None),
            P(),
            P(None, "seq", "tp"),
            P(None, "seq", "tp"),
            P(None, "seq"),
            P(None, "seq"),
            P(),
            P(),
            P(),
            P(),
        ),
        out_specs=(P(None, None, "tp"), P(None, None, "tp"), P(None, None, "tp")),
        check_vma=False,
    )
```

profile of v0, /device:TPU:8, one launch (start us, length us, event | category | flops | bytes accessed | tf_op | source)
XLA Modules:
  0.0 712.5 jit_solution(17226373592038998446)
XLA Ops:
  8.7 10.5 %all-reduce.3 = (f32[4]{0:T(128)S(1)}, f32[4]{0:T(128)S(1)}, f32[4]{0:T(128)S(1)}, f32[4]{0:T(128)S(1)}) all-reduce(f32[4]{0:T(128)S(1)} %fusion.94, f32[4]{0:T(128)S(1)} %fusion.106, f32[4]{0:T(128)S(1)} %fusion.102, f32[4]{0:T(128)S(1)} %fusion.98), channel_id=1, replica_groups=mesh['seq'=64,'tp'=4] {'tp'}, use_global_device_ids=true, to_apply=%region_1.0 | all-reduce | flops 16 | bytes 128 | tf_op jit(solution)/shard_map/psum | solution.py:89
  20.1 10.4 %all_gather.24 = bf16[4,1024]{1,0:T(4,128)(2,1)S(1)} all-gather(bf16[4,256]{1,0:T(4,128)(2,1)S(1)} %get-tuple-element.136), channel_id=1, replica_groups=mesh['seq'=64,'tp'=4] {'tp'}, dimensions={1}, use_global_device_ids=true | all-gather | bytes 10240 | tf_op jit(solution)/shard_map/all_gather | solution.py:94
  32.9 10.5 %all_gather.26 = bf16[4,1024]{1,0:T(4,128)(2,1)S(1)} all-gather(bf16[4,256]{1,0:T(4,128)(2,1)S(1)} %get-tuple-element.137), channel_id=1, replica_groups=mesh['seq'=64,'tp'=4] {'tp'}, dimensions={1}, use_global_device_ids=true | all-gather | bytes 10240 | tf_op jit(solution)/shard_map/all_gather | solution.py:94
  46.2 10.4 %all_gather.28 = bf16[4,1024]{1,0:T(4,128)(2,1)S(1)} all-gather(bf16[4,256]{1,0:T(4,128)(2,1)S(1)} %get-tuple-element.138), channel_id=1, replica_groups=mesh['seq'=64,'tp'=4] {'tp'}, dimensions={1}, use_global_device_ids=true | all-gather | bytes 10240 | tf_op jit(solution)/shard_map/all_gather | solution.py:94
  57.1 10.5 %all_gather.30 = bf16[4,1024]{1,0:T(4,128)(2,1)S(1)} all-gather(bf16[4,256]{1,0:T(4,128)(2,1)S(1)} %get-tuple-element.139), channel_id=1, replica_groups=mesh['seq'=64,'tp'=4] {'tp'}, dimensions={1}, use_global_device_ids=true | all-gather | bytes 10240 | tf_op jit(solution)/shard_map/all_gather | solution.py:94
  75.8 108.2 %all-reduce.1 = (f32[4,4]{1,0:T(4,128)S(1)}, f32[4,4]{1,0:T(4,128)S(1)}, f32[4,4]{1,0:T(4,128)S(1)}, f32[4,4]{1,0:T(4,128)S(1)}) all-reduce(f32[4,4]{1,0:T(4,128)S(1)} %get-tuple-element.78, f32[4,4]{1,0:T(4,128)S(1)} %get-tuple-element.125, f32[4,4]{1,0:T(4,128)S(1)} %get-tuple-element.123, ...), channel_id=1, replica_groups=mesh['seq'=64,'tp'=4] {'seq'}, use_global_device_ids=true, to_apply=%region_40.41 | all-reduce | flops 64 | bytes 512 | tf_op jit(solution)/shard_map/pmax | solution.py:127
  184.6 1.7 fusion.14
  189.5 231.8 %all-reduce = (f32[4,4]{1,0:T(4,128)S(1)}, f32[4,256]{1,0:T(4,128)S(1)}, f32[4,4]{1,0:T(4,128)S(1)}, f32[4,256]{1,0:T(4,128)S(1)}, f32[4,4]{1,0:T(4,128)S(1)}, /...) all-reduce(f32[4,4]{1,0:T(4,128)S(1)} %get-tuple-element.70, ...), channel_id=1, replica_groups=mesh['seq'=64,'tp'=4] {'seq'}, use_global_device_ids=true, to_apply=%region_44.45 | all-reduce | flops 4160 | bytes 33280 | tf_op jit(solution)/shard_map/psum | solution.py:129
  432.0 43.5 %reduce-scatter.37.cloned.1.call-done = f32[256,4]{1,0:T(8,128)} async-done(((f32[1024,4]{1,0:T(8,128)}), f32[256,4]{1,0:T(8,128)}) %reduce-scatter.37.cloned.1.call-update) | async-done | bytes 4112
  476.5 25.3 %reduce-scatter.33.cloned.1.call-done = f32[256,4]{1,0:T(8,128)} async-done(((f32[1024,4]{1,0:T(8,128)}), f32[256,4]{1,0:T(8,128)}) %reduce-scatter.33.cloned.1.call-update) | async-done | bytes 4112
  502.7 25.3 %reduce-scatter.29.cloned.1.call-done = f32[256,4]{1,0:T(8,128)} async-done(((f32[1024,4]{1,0:T(8,128)}), f32[256,4]{1,0:T(8,128)}) %reduce-scatter.29.cloned.1.call-update) | async-done | bytes 4112
  529.0 25.2 %reduce-scatter.25.cloned.1.call-done = f32[256,4]{1,0:T(8,128)} async-done(((f32[1024,4]{1,0:T(8,128)}), f32[256,4]{1,0:T(8,128)}) %reduce-scatter.25.cloned.1.call-update) | async-done | bytes 4112
  555.5 8.4 %all-reduce.2 = (f32[4]{0:T(128)S(1)}, f32[4]{0:T(128)S(1)}, f32[4]{0:T(128)S(1)}, f32[4]{0:T(128)S(1)}) all-reduce(f32[4]{0:T(128)S(1)} %get-tuple-element.156, f32[4]{0:T(128)S(1)} %get-tuple-element.54, f32[4]{0:T(128)S(1)} %get-tuple-element.154, f32[4]{0:T(128)S(1)} %get-tuple-element.47), channel_id=1, replica_groups=mesh['seq'=64,'tp'=4] {'tp'}, use_global_device_ids=true, to_apply=%region_48.49 | all-reduce | flops 16 | bytes 128 | tf_op jit(solution)/shard_map/psum | solution.py:157
  564.0 10.4 %all_gather.25 = bf16[4,1024]{1,0:T(4,128)(2,1)S(1)} all-gather(bf16[4,256]{1,0:T(4,128)(2,1)S(1)} %get-tuple-element.130), channel_id=1, replica_groups=mesh['seq'=64,'tp'=4] {'tp'}, dimensions={1}, use_global_device_ids=true | all-gather | bytes 10240 | tf_op jit(solution)/shard_map/all_gather | solution.py:162
  574.4 10.4 %all_gather.27 = bf16[4,1024]{1,0:T(4,128)(2,1)S(1)} all-gather(bf16[4,256]{1,0:T(4,128)(2,1)S(1)} %get-tuple-element.131), channel_id=1, replica_groups=mesh['seq'=64,'tp'=4] {'tp'}, dimensions={1}, use_global_device_ids=true | all-gather | bytes 10240 | tf_op jit(solution)/shard_map/all_gather | solution.py:162
  584.8 10.4 %all_gather.29 = bf16[4,1024]{1,0:T(4,128)(2,1)S(1)} all-gather(bf16[4,256]{1,0:T(4,128)(2,1)S(1)} %get-tuple-element.132), channel_id=1, replica_groups=mesh['seq'=64,'tp'=4] {'tp'}, dimensions={1}, use_global_device_ids=true | all-gather | bytes 10240 | tf_op jit(solution)/shard_map/all_gather | solution.py:162
  596.3 4.1 convolution_bitcast_fusion.3
  600.7 4.1 convolution_bitcast_fusion.2
  604.8 4.1 convolution_bitcast_fusion.1
  608.8 10.5 %all_gather.31 = bf16[4,1024]{1,0:T(4,128)(2,1)S(1)} all-gather(bf16[4,256]{1,0:T(4,128)(2,1)S(1)} %get-tuple-element.133), channel_id=1, replica_groups=mesh['seq'=64,'tp'=4] {'tp'}, dimensions={1}, use_global_device_ids=true | all-gather | bytes 10240 | tf_op jit(solution)/shard_map/all_gather | solution.py:162
  620.1 4.1 convolution_bitcast_fusion
  626.3 25.2 %reduce-scatter.31.cloned.1.call-done = f32[256,4]{1,0:T(8,128)} async-done(((f32[1024,4]{1,0:T(8,128)}), f32[256,4]{1,0:T(8,128)}) %reduce-scatter.31.cloned.1.call-update) | async-done | bytes 4112
  652.4 25.3 %reduce-scatter.35.cloned.1.call-done = f32[256,4]{1,0:T(8,128)} async-done(((f32[1024,4]{1,0:T(8,128)}), f32[256,4]{1,0:T(8,128)}) %reduce-scatter.35.cloned.1.call-update) | async-done | bytes 4112
  678.7 25.3 %reduce-scatter.39.cloned.1.call-done = f32[256,4]{1,0:T(8,128)} async-done(((f32[1024,4]{1,0:T(8,128)}), f32[256,4]{1,0:T(8,128)}) %reduce-scatter.39.cloned.1.call-update) | async-done | bytes 4112
  (226 shorter events, 42.8 us)
Async XLA Ops:
  7.2 588.0 %copy-start = (bf16[1024,1024]{1,0:T(8,128)(2,1)S(1)}, bf16[1024,1024]{1,0:T(8,128)(2,1)}, u32[]{:S(2)}) copy-start(bf16[1024,1024]{1,0:T(8,128)(2,1)} %param.26) | copy-start | bytes 6291460
  7.2 49.4 %copy-start.1 = (bf16[1024,256]{1,0:T(8,128)(2,1)S(1)}, bf16[1024,256]{1,0:T(8,128)(2,1)}, u32[]{:S(2)}) copy-start(bf16[1024,256]{1,0:T(8,128)(2,1)} %param.24) | copy-start | bytes 1572868
  7.2 49.6 %copy-start.2 = (bf16[1024,256]{1,0:T(8,128)(2,1)S(1)}, bf16[1024,256]{1,0:T(8,128)(2,1)}, u32[]{:S(2)}) copy-start(bf16[1024,256]{1,0:T(8,128)(2,1)} %param.23) | copy-start | bytes 1572868
  7.2 468.3 %reduce-scatter.37.cloned.1.call-start = ((), (), s32[]{:S(2)}) async-start(), calls=%async_computation.14 | async-start | bytes 655360
  19.2 26.6 %copy-start.3 = (bf16[1024,256]{1,0:T(8,128)(2,1)S(1)}, bf16[1024,256]{1,0:T(8,128)(2,1)}, u32[]{:S(2)}) copy-start(bf16[1024,256]{1,0:T(8,128)(2,1)} %param.22) | copy-start | bytes 1572868
  45.8 22.3 %copy-start.11 = (f32[2,16]{1,0:T(2,128)S(1)}, f32[2,16]{1,0:T(2,128)}, u32[]{:S(2)}) copy-start(f32[2,16]{1,0:T(2,128)} %param.29) | copy-start | bytes 388
  45.8 22.4 %copy-start.14 = (s32[4]{0:T(128)S(1)}, s32[4]{0:T(128)}, u32[]{:S(2)}) copy-start(s32[4]{0:T(128)} %param.35) | copy-start | bytes 52
  45.8 22.4 %copy-start.8 = (s32[4,4]{1,0:T(4,128)S(1)}, s32[4,4]{1,0:T(4,128)}, u32[]{:S(2)}) copy-start(s32[4,4]{1,0:T(4,128)} %param.37) | copy-start | bytes 196
  45.8 22.6 %copy-start.7 = (s32[4,4]{1,0:T(4,128)S(1)}, s32[4,4]{1,0:T(4,128)}, u32[]{:S(2)}) copy-start(s32[4,4]{1,0:T(4,128)} %param.36) | copy-start | bytes 196
  73.3 2.1 copy-start.10
  73.3 2.1 copy-start.13
  73.3 2.2 copy-start.9
  75.4 108.8 %copy-start.5 = (bf16[4,512,256]{1,2,0:T(8,128)(2,1)}, bf16[4,512,256]{1,2,0:T(8,128)(2,1)S(1)}, u32[]{:S(2)}) copy-start(bf16[4,512,256]{1,2,0:T(8,128)(2,1)S(1)} %copy.48) | copy-start | bytes 3145732
  184.6 3.3 copy-start.6
  184.6 237.2 %copy-start.4 = (bf16[256,1024]{1,0:T(8,128)(2,1)S(1)}, bf16[256,1024]{1,0:T(8,128)(2,1)}, u32[]{:S(2)}) copy-start(bf16[256,1024]{1,0:T(8,128)(2,1)} %param.25) | copy-start | bytes 1572868
  423.0 78.7 %reduce-scatter.33.cloned.1.call-start = ((), (), s32[]{:S(2)}) async-start(), calls=%async_computation.12 | async-start | bytes 655360
  425.7 5.1 copy-start.12
  425.7 102.4 %reduce-scatter.29.cloned.1.call-start = ((), (), s32[]{:S(2)}) async-start(), calls=%async_computation.10 | async-start | bytes 655360
  428.4 125.8 %reduce-scatter.25.cloned.1.call-start = ((), (), s32[]{:S(2)}) async-start(), calls=%async_computation.8 | async-start | bytes 655360
  430.3 195.0 %reduce-scatter.27.cloned.1.call-start = ((), (), s32[]{:S(2)}) async-start(), calls=%async_computation.9 | async-start | bytes 655360
  600.5 51.0 %reduce-scatter.31.cloned.1.call-start = ((), (), s32[]{:S(2)}) async-start(), calls=%async_computation.11 | async-start | bytes 655360
  619.3 58.4 %reduce-scatter.35.cloned.1.call-start = ((), (), s32[]{:S(2)}) async-start(), calls=%async_computation.13 | async-start | bytes 655360
  620.1 84.0 %reduce-scatter.39.cloned.1.call-start = ((), (), s32[]{:S(2)}) async-start(), calls=%async_computation.15 | async-start | bytes 655360
Sparse Core Ops, SparseCore 0:
  423.1 52.3 reduce-scatter.36
  478.1 23.6 reduce-scatter.32
  504.3 23.7 reduce-scatter.28
  530.4 23.7 reduce-scatter.24
  600.6 24.6 reduce-scatter.26
  627.7 23.7 reduce-scatter.30
  654.0 23.7 reduce-scatter.34
  680.3 23.7 reduce-scatter.38
where the time goes:
time: 713 us; the launch traced here: 712 us
  blocking collectives  442 us (62%)
  waiting for transfers between devices  196 us (27%)
  matrix products  34.7 us (5%)
  local copies, waits for them, and re-layouts  18.9 us (3%)
  between operations  14.5 us (2%)
    psum x1, blocking collectives, on_device(): lax.psum((local_total * factor, local_sum * jnp.repeat(factor, HEAD_DIM,...  232 us
    unnamed x16, waiting for transfers between devices  196 us
    pmax x1, blocking collectives, on_device(): peak_all = lax.pmax(local_peak, 'seq')  108 us
    all_gather x4, blocking collectives, on_device(): normed = lax.all_gather(normed_local, 'tp', axis=1, tiled=True)  41.7 us
    all_gather x4, blocking collectives, on_device(): normed_two = lax.all_gather(normed_two_local, 'tp', axis=1, tiled=True)  41.6 us
    unnamed x8, matrix products  21 us
  transfers between devices with their start and end apart: 8, of which 8 were waited for; matrix products, arithmetic and copies ran while one was open for 4% of the time, Pallas kernels for 0%

commit v1 on v0

--- a/solution.py
+++ b/solution.py
@@ -8,6 +8,12 @@
 HEAD_DIM = 64
 STEPS = 4
 epsilon = 1e-05
+
+
+def joined_along(pieces, dim):
+    dims = list(pieces.shape[1:])
+    dims[dim] *= pieces.shape[0]
+    return jnp.moveaxis(pieces, 0, dim).reshape(dims)
 
 
 def rotated(blocks, times):
@@ -159,7 +165,19 @@
         normed_two_local = (middle_local * second_rms[:, None] * gain_second_local).astype(
             jnp.bfloat16
         )
-        normed_two = lax.all_gather(normed_two_local, "tp", axis=1, tiled=True)
+        peers = lax.axis_size("tp")
+        pairs = [(i, (i + 1) % peers) for i in range(peers)]
+        back = [(b, a) for a, b in pairs]
+        lower, upper = ([], [])
+        for step in range(peers - 1):
+            if step % 2 == 0:
+                lower.append(lax.ppermute(lower[-1] if lower else normed_two_local, "tp", pairs))
+            else:
+                upper.append(lax.ppermute(upper[-1] if upper else normed_two_local, "tp", back))
+        pieces = jnp.stack([*lower[::-1], normed_two_local, *upper])
+        shift = lax.axis_index("tp") - len(lower)
+        pieces = pieces[(jnp.arange(peers) - shift) % peers]
+        normed_two = joined_along(pieces, 1)
         gate_part = jnp.dot(normed_two, gate_weight, preferred_element_type=jnp.float32)
         up_part = jnp.dot(normed_two, up_weight, preferred_element_type=jnp.float32)
         activated = (jax.nn.silu(gate_part) * up_part).astype(jnp.bfloat16)

time: 713 us -> 698 us (0.979)
  blocking collectives: 442 us -> 401 us
  starting transfers between devices: 0.51 us -> 15.1 us
  waiting for transfers between devices: 196 us -> 205 us
    all_gather x4 -> x0, blocking collectives: 41.6 us -> none  [on_device(): normed_two = lax.all_gather(normed_two_local, 'tp', axis=1, tiled=True)]
    ppermute x0 -> x12, starting transfers between devices: none -> 14.7 us  [the longest x4 11.7 us: on_device(): lax.ppermute(upper[-1] if upper else normed_two_local, 'tp', back)]
  transfers between devices with their start and end apart: 8 -> 20, of which waited for: 8 -> 9; matrix products, arithmetic and copies ran while one was open for 4% -> 5% of each run, Pallas kernels for 0% -> 0%
where the time goes in v1:
time: 698 us; the launch traced here: 697 us
  blocking collectives  401 us (57%)
  waiting for transfers between devices  205 us (29%)
  matrix products  35.8 us (5%)
  local copies, waits for them, and re-layouts  21.1 us (3%)
  starting transfers between devices  15.1 us (2%)
  between operations  14.5 us (2%)
    psum x1, blocking collectives, on_device(): lax.psum((local_total * factor, local_sum * jnp.repeat(factor, HEAD_DIM,...  232 us
    unnamed x16, waiting for transfers between devices  203 us
    pmax x1, blocking collectives, on_device(): peak_all = lax.pmax(local_peak, 'seq')  108 us
    all_gather x4, blocking collectives, on_device(): normed = lax.all_gather(normed_local, 'tp', axis=1, tiled=True)  41.6 us
    unnamed x8, matrix products  21 us
  transfers between devices with their start and end apart: 20, of which 9 were waited for; matrix products, arithmetic and copies ran while one was open for 5% of the time, Pallas kernels for 0%

profile of v1, /device:TPU:8, one launch (start us, length us, event | category | flops | bytes accessed | tf_op | source)
XLA Modules:
  0.0 697.0 jit_solution(3371172469275032450)
XLA Ops:
  8.7 10.5 %all-reduce.3 = (f32[4]{0:T(128)S(1)}, f32[4]{0:T(128)S(1)}, f32[4]{0:T(128)S(1)}, f32[4]{0:T(128)S(1)}) all-reduce(f32[4]{0:T(128)S(1)} %fusion.94, f32[4]{0:T(128)S(1)} %fusion.106, f32[4]{0:T(128)S(1)} %fusion.102, f32[4]{0:T(128)S(1)} %fusion.98), channel_id=1, replica_groups=mesh['seq'=64,'tp'=4] {'tp'}, use_global_device_ids=true, to_apply=%region_1.0 | all-reduce | flops 16 | bytes 128 | tf_op jit(solution)/shard_map/psum | solution.py:95
  20.0 10.4 %all_gather.12 = bf16[4,1024]{1,0:T(4,128)(2,1)S(1)} all-gather(bf16[4,256]{1,0:T(4,128)(2,1)S(1)} %get-tuple-element.136), channel_id=1, replica_groups=mesh['seq'=64,'tp'=4] {'tp'}, dimensions={1}, use_global_device_ids=true | all-gather | bytes 10240 | tf_op jit(solution)/shard_map/all_gather | solution.py:100
  30.4 10.4 %all_gather.13 = bf16[4,1024]{1,0:T(4,128)(2,1)S(1)} all-gather(bf16[4,256]{1,0:T(4,128)(2,1)S(1)} %get-tuple-element.137), channel_id=1, replica_groups=mesh['seq'=64,'tp'=4] {'tp'}, dimensions={1}, use_global_device_ids=true | all-gather | bytes 10240 | tf_op jit(solution)/shard_map/all_gather | solution.py:100
  45.8 10.4 %all_gather.14 = bf16[4,1024]{1,0:T(4,128)(2,1)S(1)} all-gather(bf16[4,256]{1,0:T(4,128)(2,1)S(1)} %get-tuple-element.138), channel_id=1, replica_groups=mesh['seq'=64,'tp'=4] {'tp'}, dimensions={1}, use_global_device_ids=true | all-gather | bytes 10240 | tf_op jit(solution)/shard_map/all_gather | solution.py:100
  56.6 10.5 %all_gather.15 = bf16[4,1024]{1,0:T(4,128)(2,1)S(1)} all-gather(bf16[4,256]{1,0:T(4,128)(2,1)S(1)} %get-tuple-element.139), channel_id=1, replica_groups=mesh['seq'=64,'tp'=4] {'tp'}, dimensions={1}, use_global_device_ids=true | all-gather | bytes 10240 | tf_op jit(solution)/shard_map/all_gather | solution.py:100
  75.8 108.2 %all-reduce.1 = (f32[4,4]{1,0:T(4,128)S(1)}, f32[4,4]{1,0:T(4,128)S(1)}, f32[4,4]{1,0:T(4,128)S(1)}, f32[4,4]{1,0:T(4,128)S(1)}) all-reduce(f32[4,4]{1,0:T(4,128)S(1)} %get-tuple-element.78, f32[4,4]{1,0:T(4,128)S(1)} %get-tuple-element.125, f32[4,4]{1,0:T(4,128)S(1)} %get-tuple-element.123, ...), channel_id=1, replica_groups=mesh['seq'=64,'tp'=4] {'seq'}, use_global_device_ids=true, to_apply=%region_40.41 | all-reduce | flops 64 | bytes 512 | tf_op jit(solution)/shard_map/pmax | solution.py:133
  190.6 231.8 %all-reduce = (f32[4,4]{1,0:T(4,128)S(1)}, f32[4,256]{1,0:T(4,128)S(1)}, f32[4,4]{1,0:T(4,128)S(1)}, f32[4,256]{1,0:T(4,128)S(1)}, f32[4,4]{1,0:T(4,128)S(1)}, /...) all-reduce(f32[4,4]{1,0:T(4,128)S(1)} %get-tuple-element.70, ...), channel_id=1, replica_groups=mesh['seq'=64,'tp'=4] {'seq'}, use_global_device_ids=true, to_apply=%region_44.45 | all-reduce | flops 4160 | bytes 33280 | tf_op jit(solution)/shard_map/psum | solution.py:135
  431.9 44.7 %reduce-scatter.37.cloned.1.call-done = f32[256,4]{1,0:T(8,128)} async-done(((f32[1024,4]{1,0:T(8,128)}), f32[256,4]{1,0:T(8,128)}) %reduce-scatter.37.cloned.1.call-update) | async-done | bytes 4112
  477.6 25.3 %reduce-scatter.33.cloned.1.call-done = f32[256,4]{1,0:T(8,128)} async-done(((f32[1024,4]{1,0:T(8,128)}), f32[256,4]{1,0:T(8,128)}) %reduce-scatter.33.cloned.1.call-update) | async-done | bytes 4112
  503.8 25.3 %reduce-scatter.29.cloned.1.call-done = f32[256,4]{1,0:T(8,128)} async-done(((f32[1024,4]{1,0:T(8,128)}), f32[256,4]{1,0:T(8,128)}) %reduce-scatter.29.cloned.1.call-update) | async-done | bytes 4112
  530.1 25.2 %reduce-scatter.25.cloned.1.call-done = f32[256,4]{1,0:T(8,128)} async-done(((f32[1024,4]{1,0:T(8,128)}), f32[256,4]{1,0:T(8,128)}) %reduce-scatter.25.cloned.1.call-update) | async-done | bytes 4112
  556.6 8.4 %all-reduce.2 = (f32[4]{0:T(128)S(1)}, f32[4]{0:T(128)S(1)}, f32[4]{0:T(128)S(1)}, f32[4]{0:T(128)S(1)}) all-reduce(f32[4]{0:T(128)S(1)} %get-tuple-element.156, f32[4]{0:T(128)S(1)} %get-tuple-element.54, f32[4]{0:T(128)S(1)} %get-tuple-element.154, f32[4]{0:T(128)S(1)} %get-tuple-element.47), channel_id=1, replica_groups=mesh['seq'=64,'tp'=4] {'tp'}, use_global_device_ids=true, to_apply=%region_48.49 | all-reduce | flops 16 | bytes 128 | tf_op jit(solution)/shard_map/psum | solution.py:163
  566.5 2.0 collective-permute-start.2
  571.3 3.1 collective-permute-start.5
  574.4 3.2 collective-permute-start.8
  578.7 4.1 convolution_bitcast_fusion.3
  582.9 3.3 collective-permute-start.11
  588.6 4.1 convolution_bitcast_fusion.2
  593.7 4.1 convolution_bitcast_fusion.1
  599.2 4.1 convolution_bitcast_fusion
  603.3 6.6 reduce-scatter.27.cloned.1.call-done
  610.8 25.2 %reduce-scatter.31.cloned.1.call-done = f32[256,4]{1,0:T(8,128)} async-done(((f32[1024,4]{1,0:T(8,128)}), f32[256,4]{1,0:T(8,128)}) %reduce-scatter.31.cloned.1.call-update) | async-done | bytes 4112
  636.9 25.3 %reduce-scatter.35.cloned.1.call-done = f32[256,4]{1,0:T(8,128)} async-done(((f32[1024,4]{1,0:T(8,128)}), f32[256,4]{1,0:T(8,128)}) %reduce-scatter.35.cloned.1.call-update) | async-done | bytes 4112
  663.2 25.3 %reduce-scatter.39.cloned.1.call-done = f32[256,4]{1,0:T(8,128)} async-done(((f32[1024,4]{1,0:T(8,128)}), f32[256,4]{1,0:T(8,128)}) %reduce-scatter.39.cloned.1.call-update) | async-done | bytes 4112
  (254 shorter events, 51.2 us)
Async XLA Ops:
  7.2 571.2 %copy-start = (bf16[1024,1024]{1,0:T(8,128)(2,1)S(1)}, bf16[1024,1024]{1,0:T(8,128)(2,1)}, u32[]{:S(2)}) copy-start(bf16[1024,1024]{1,0:T(8,128)(2,1)} %param.26) | copy-start | bytes 6291460
  7.2 49.2 %copy-start.2 = (bf16[1024,256]{1,0:T(8,128)(2,1)S(1)}, bf16[1024,256]{1,0:T(8,128)(2,1)}, u32[]{:S(2)}) copy-start(bf16[1024,256]{1,0:T(8,128)(2,1)} %param.24) | copy-start | bytes 1572868
  7.2 469.4 %reduce-scatter.37.cloned.1.call-start = ((), (), s32[]{:S(2)}) async-start(), calls=%async_computation.14 | async-start | bytes 655360
  75.4 108.8 %copy-start.5 = (bf16[4,512,256]{1,2,0:T(8,128)(2,1)}, bf16[4,512,256]{1,2,0:T(8,128)(2,1)S(1)}, u32[]{:S(2)}) copy-start(bf16[4,512,256]{1,2,0:T(8,128)(2,1)S(1)} %copy.48) | copy-start | bytes 3145732
  184.6 238.3 %copy-start.4 = (bf16[256,1024]{1,0:T(8,128)(2,1)S(1)}, bf16[256,1024]{1,0:T(8,128)(2,1)}, u32[]{:S(2)}) copy-start(bf16[256,1024]{1,0:T(8,128)(2,1)} %param.25) | copy-start | bytes 1572868
  424.1 78.7 %reduce-scatter.33.cloned.1.call-start = ((), (), s32[]{:S(2)}) async-start(), calls=%async_computation.12 | async-start | bytes 655360
  426.8 102.4 %reduce-scatter.29.cloned.1.call-start = ((), (), s32[]{:S(2)}) async-start(), calls=%async_computation.10 | async-start | bytes 655360
  429.4 125.8 %reduce-scatter.25.cloned.1.call-start = ((), (), s32[]{:S(2)}) async-start(), calls=%async_computation.8 | async-start | bytes 655360
  431.4 178.4 %reduce-scatter.27.cloned.1.call-start = ((), (), s32[]{:S(2)}) async-start(), calls=%async_computation.9 | async-start | bytes 655360
  565.1 4.8 collective-permute-start
  566.5 7.9 %collective-permute-start.2 = (bf16[4,256]{1,0:T(4,128)(2,1)S(1)}, bf16[4,256]{1,0:T(4,128)(2,1)S(1)}, u32[]{:S(2)}, u32[]{:S(2)}) collective-permute-start(bf16[4,256]{1,0:T(4,128)(2,1)S(1)} %get-tuple-element.130), channel_id=1, source_target_pairs={{1,0},{2,1},{3,2},{0,3},{5,4},{6,5},{7,6},{4,7},{9,8},{10,9},{11,1... | collective-permute-start | bytes 6152 | tf_op jit(solution)/shard_map/ppermute | solution.py:176
  568.5 9.2 %collective-permute-start.3 = (bf16[4,256]{1,0:T(4,128)(2,1)S(1)}, bf16[4,256]{1,0:T(4,128)(2,1)S(1)}, u32[]{:S(2)}, u32[]{:S(2)}) collective-permute-start(bf16[4,256]{1,0:T(4,128)(2,1)S(1)} %get-tuple-element.131), channel_id=1, source_target_pairs={{0,1},{1,2},{2,3},{3,0},{4,5},{5,6},{6,7},{7,4},{8,9},{9,10},{10,1... | collective-permute-start | bytes 6152 | tf_op jit(solution)/shard_map/ppermute | solution.py:174
  569.9 7.7 %collective-permute-start.1 = (bf16[4,256]{1,0:T(4,128)(2,1)S(1)}, bf16[4,256]{1,0:T(4,128)(2,1)S(1)}, u32[]{:S(2)}, u32[]{:S(2)}) collective-permute-start(bf16[4,256]{1,0:T(4,128)(2,1)S(1)} %collective-permute-done), channel_id=1, source_target_pairs={{0,1},{1,2},{2,3},{3,0},{4,5},{5,6},{6,7},{7,4},{8,9},{9,10},{10,1... | collective-permute-start | bytes 6152 | tf_op jit(solution)/shard_map/ppermute | solution.py:174
  571.3 11.6 %collective-permute-start.5 = (bf16[4,256]{1,0:T(4,128)(2,1)S(1)}, bf16[4,256]{1,0:T(4,128)(2,1)S(1)}, u32[]{:S(2)}, u32[]{:S(2)}) collective-permute-start(bf16[4,256]{1,0:T(4,128)(2,1)S(1)} %get-tuple-element.131), channel_id=1, source_target_pairs={{1,0},{2,1},{3,2},{0,3},{5,4},{6,5},{7,6},{4,7},{9,8},{10,9},{11,1... | collective-permute-start | bytes 6152 | tf_op jit(solution)/shard_map/ppermute | solution.py:176
  574.4 11.8 %collective-permute-start.6 = (bf16[4,256]{1,0:T(4,128)(2,1)S(1)}, bf16[4,256]{1,0:T(4,128)(2,1)S(1)}, u32[]{:S(2)}, u32[]{:S(2)}) collective-permute-start(bf16[4,256]{1,0:T(4,128)(2,1)S(1)} %get-tuple-element.132), channel_id=1, source_target_pairs={{0,1},{1,2},{2,3},{3,0},{4,5},{5,6},{6,7},{7,4},{8,9},{9,10},{10,1... | collective-permute-start | bytes 6152 | tf_op jit(solution)/shard_map/ppermute | solution.py:174
  574.4 18.3 %collective-permute-start.8 = (bf16[4,256]{1,0:T(4,128)(2,1)S(1)}, bf16[4,256]{1,0:T(4,128)(2,1)S(1)}, u32[]{:S(2)}, u32[]{:S(2)}) collective-permute-start(bf16[4,256]{1,0:T(4,128)(2,1)S(1)} %get-tuple-element.132), channel_id=1, source_target_pairs={{1,0},{2,1},{3,2},{0,3},{5,4},{6,5},{7,6},{4,7},{9,8},{10,9},{11,1... | collective-permute-start | bytes 6152 | tf_op jit(solution)/shard_map/ppermute | solution.py:176
  577.6 8.6 %collective-permute-start.9 = (bf16[4,256]{1,0:T(4,128)(2,1)S(1)}, bf16[4,256]{1,0:T(4,128)(2,1)S(1)}, u32[]{:S(2)}, u32[]{:S(2)}) collective-permute-start(bf16[4,256]{1,0:T(4,128)(2,1)S(1)} %get-tuple-element.133), channel_id=1, source_target_pairs={{0,1},{1,2},{2,3},{3,0},{4,5},{5,6},{6,7},{7,4},{8,9},{9,10},{10,1... | collective-permute-start | bytes 6152 | tf_op jit(solution)/shard_map/ppermute | solution.py:174
  577.6 10.0 %collective-permute-start.4 = (bf16[4,256]{1,0:T(4,128)(2,1)S(1)}, bf16[4,256]{1,0:T(4,128)(2,1)S(1)}, u32[]{:S(2)}, u32[]{:S(2)}) collective-permute-start(bf16[4,256]{1,0:T(4,128)(2,1)S(1)} %collective-permute-done.3), channel_id=1, source_target_pairs={{0,1},{1,2},{2,3},{3,0},{4,5},{5,6},{6,7},{7,4},{8,9},{9,10},{10,1... | collective-permute-start | bytes 6152 | tf_op jit(solution)/shard_map/ppermute | solution.py:174
  582.8 53.1 %reduce-scatter.31.cloned.1.call-start = ((), (), s32[]{:S(2)}) async-start(), calls=%async_computation.11 | async-start | bytes 655360
  582.9 14.8 %collective-permute-start.11 = (bf16[4,256]{1,0:T(4,128)(2,1)S(1)}, bf16[4,256]{1,0:T(4,128)(2,1)S(1)}, u32[]{:S(2)}, u32[]{:S(2)}) collective-permute-start(bf16[4,256]{1,0:T(4,128)(2,1)S(1)} %get-tuple-element.133), channel_id=1, source_target_pairs={{1,0},{2,1},{3,2},{0,3},{5,4},{6,5},{7,6},{4,7},{9,8},{10,9},{11,1... | collective-permute-start | bytes 6152 | tf_op jit(solution)/shard_map/ppermute | solution.py:176
  586.2 6.5 collective-permute-start.7
  586.2 11.5 %collective-permute-start.10 = (bf16[4,256]{1,0:T(4,128)(2,1)S(1)}, bf16[4,256]{1,0:T(4,128)(2,1)S(1)}, u32[]{:S(2)}, u32[]{:S(2)}) collective-permute-start(bf16[4,256]{1,0:T(4,128)(2,1)S(1)} %collective-permute-done.9), channel_id=1, source_target_pairs={{0,1},{1,2},{2,3},{3,0},{4,5},{5,6},{6,7},{7,4},{8,9},{9,10},{10,1... | collective-permute-start | bytes 6152 | tf_op jit(solution)/shard_map/ppermute | solution.py:174
  598.4 63.9 %reduce-scatter.35.cloned.1.call-start = ((), (), s32[]{:S(2)}) async-start(), calls=%async_computation.13 | async-start | bytes 655360
  599.1 89.4 %reduce-scatter.39.cloned.1.call-start = ((), (), s32[]{:S(2)}) async-start(), calls=%async_computation.15 | async-start | bytes 655360
  (10 other events, 126.8 us)
Sparse Core Ops, SparseCore 0:
  424.2 52.3 reduce-scatter.36
  479.1 23.6 reduce-scatter.32
  505.4 23.7 reduce-scatter.28
  531.5 23.7 reduce-scatter.24
  582.9 26.8 reduce-scatter.26
  612.2 23.7 reduce-scatter.30
  638.5 23.7 reduce-scatter.34
  664.8 23.7 reduce-scatter.38
